TPU v7x, 512 devices: a whole 4x4x16 slice. The times are simulated.
512 devices in a mesh: gx: 8 (over y, core), gy: 4 (over x), gz: 16 (over z).
Axes of the slice: x: 4, y: 4, z: 16, core: 2. Of those that a mesh axis runs over, the one named last changes fastest.
Arguments:
- level_set: float32 [128, 64, 2048], P('gx', 'gy', 'gz'), may hold values from 0 to 1
- velocity: float32 [3, 128, 64, 2048], P(None, 'gx', 'gy', 'gz'), may hold values from -6 to 6
- source: float32 [128, 64, 2048], P('gx', 'gy', 'gz'), may hold values from -6 to 6
- coarse_factor: float32 [512, 512], P(('gx', 'gy', 'gz')), may hold values from -0.2 to 0.2
Outputs:
- level_set_new: float32 [128, 64, 2048], P('gx', 'gy', 'gz')
- pressure: float32 [128, 64, 2048], P('gx', 'gy', 'gz')
All inputs are finite; a program needn't handle non-finite values.
Results may differ from a plain program's by a relative error of at most 0.029.
Values sent between devices are 32-bit elements; how exact they have to be, the bound alone decides.
A program may use at most 64 MiB of HBM per device.

v0:
```python
import jax
import jax.numpy as jnp
import numpy as np
from jax import lax
from jax.sharding import PartitionSpec as P

NP = 8
RSWEEPS = 2
ITERS = 6
GLL_POINTS = (
    -1.0,
    -0.8717401485096066,
    -0.5917001814331423,
    -0.2092992179024789,
    0.2092992179024789,
    0.5917001814331423,
    0.8717401485096066,
    1.0,
)
GLL_WEIGHTS = (
    0.03571428571428571,
    0.21070422714350603,
    0.3411226924835044,
    0.4124587946587038,
    0.4124587946587038,
    0.3411226924835044,
    0.21070422714350603,
    0.03571428571428571,
)
HIGHEST = lax.Precision.HIGHEST
TIME_STEP = 0.02
PSEUDO_STEP = 0.004
INTERFACE_WIDTH = 0.5
GAS_DENSITY = 0.1
SOURCE_SCALE = 20.0


def extended(cells, sides, width):
    for axis, dim in sides:
        count = lax.axis_size(axis)
        ends = count - 1
        head = lax.slice_in_dim(cells, 0, width, axis=dim)
        tail = lax.slice_in_dim(cells, cells.shape[dim] - width, cells.shape[dim], axis=dim)
        cells = jnp.concatenate(
            [
                lax.ppermute(tail, axis, [(i, (i + 1) % count) for i in range(ends)]),
                cells,
                lax.ppermute(head, axis, [((i + 1) % count, i) for i in range(ends)]),
            ],
            axis=dim,
        )
    return cells


def node_tables():
    points = np.array(GLL_POINTS)
    amount = points.shape[0]
    barycentric = np.ones(amount)
    for target in range(amount):
        for partner in range(amount):
            if partner != target:
                barycentric[target] = barycentric[target] / (points[target] - points[partner])
    derivative = np.zeros((amount, amount))
    for target in range(amount):
        for partner in range(amount):
            if partner != target:
                derivative[target, partner] = (
                    barycentric[partner] / barycentric[target] / (points[target] - points[partner])
                )
        derivative[target, target] = -np.sum(derivative[target])
    return derivative


def apply_axis(values, matrix, which_axis):
    if which_axis == 0:
        return jnp.einsum("ap,pqr->aqr", matrix, values, precision=HIGHEST)
    if which_axis == 1:
        return jnp.einsum("aq,pqr->par", matrix, values, precision=HIGHEST)
    return jnp.einsum("pqr,ar->pqa", values, matrix, precision=HIGHEST)


def edge_passes(padded):
    summed = padded
    for which_axis in (1, 2, 3):
        amount = summed.shape[which_axis] - 2
        center = lax.slice_in_dim(summed, 1, amount + 1, axis=which_axis)
        upper_side = lax.slice_in_dim(summed, 2, amount + 2, axis=which_axis)
        lower_side = lax.slice_in_dim(summed, 0, amount, axis=which_axis)
        shape_list = [1, 1, 1, 1]
        shape_list[which_axis] = amount
        position = (jnp.arange(amount) % NP).reshape(shape_list)
        summed = (
            center
            + jnp.where(position == NP - 1, upper_side, 0.0)
            + jnp.where(position == 0, lower_side, 0.0)
        )
    return summed


def assemble(stacked):
    padded = extended(stacked, (("gx", 1), ("gy", 2), ("gz", 3)), 1)
    return edge_passes(padded)


def body(level_set, velocity, source, coarse_factor):
    shape_tuple = level_set.shape
    derivative = node_tables()
    deriv_tables = [
        jnp.asarray(np.kron(np.eye(extent // NP), derivative), jnp.float32)
        for extent in shape_tuple
    ]
    trans_tables = [
        jnp.asarray(np.kron(np.eye(extent // NP), derivative.T), jnp.float32)
        for extent in shape_tuple
    ]
    square_tables = [
        jnp.asarray(np.kron(np.eye(extent // NP), (derivative * derivative).T), jnp.float32)
        for extent in shape_tuple
    ]
    weights = jnp.asarray(np.array(GLL_WEIGHTS), jnp.float32)
    along_x = jnp.tile(weights, shape_tuple[0] // NP)
    along_y = jnp.tile(weights, shape_tuple[1] // NP)
    along_z = jnp.tile(weights, shape_tuple[2] // NP)
    bmass = along_x[:, None, None] * along_y[None, :, None] * along_z[None, None, :]
    gradient = [
        apply_axis(level_set, deriv_tables[which_axis], which_axis) for which_axis in range(3)
    ]
    advect = velocity[0] * gradient[0] + velocity[1] * gradient[1] + velocity[2] * gradient[2]
    divergence = (
        apply_axis(bmass * velocity[0], trans_tables[0], 0)
        + apply_axis(bmass * velocity[1], trans_tables[1], 1)
        + apply_axis(bmass * velocity[2], trans_tables[2], 2)
        + bmass * source
    )
    assembled = assemble(jnp.stack([bmass * advect, bmass, divergence]))
    mass_sum = assembled[1]
    weight = bmass / mass_sum
    level_now = level_set - TIME_STEP * assembled[0] / mass_sum
    rhs_field = SOURCE_SCALE * assembled[2]
    for sweep in range(RSWEEPS):
        gradient = [
            apply_axis(level_now, deriv_tables[which_axis], which_axis) for which_axis in range(3)
        ]
        inv_norm = 1.0 / jnp.sqrt(
            1.0 + gradient[0] * gradient[0] + gradient[1] * gradient[1] + gradient[2] * gradient[2]
        )
        compress = level_now * (1.0 - level_now) * inv_norm
        weak_form = apply_axis(
            bmass * (compress * gradient[0] - INTERFACE_WIDTH * gradient[0]), trans_tables[0], 0
        )
        weak_form = weak_form + apply_axis(
            bmass * (compress * gradient[1] - INTERFACE_WIDTH * gradient[1]), trans_tables[1], 1
        )
        weak_form = weak_form + apply_axis(
            bmass * (compress * gradient[2] - INTERFACE_WIDTH * gradient[2]), trans_tables[2], 2
        )
        level_now = level_now + PSEUDO_STEP * assemble(weak_form[None])[0] / mass_sum
    inverse_density = 1.0 / (GAS_DENSITY + (1.0 - GAS_DENSITY) * jnp.clip(level_now, 0.0, 1.0))
    scaled = bmass * inverse_density
    diag_local = (
        apply_axis(scaled, square_tables[0], 0)
        + apply_axis(scaled, square_tables[1], 1)
        + apply_axis(scaled, square_tables[2], 2)
        + bmass
    )
    diagonal = assemble(diag_local[None])[0]
    own_row = coarse_factor[0]

    def precondition(residual):
        jacobi = residual / diagonal
        restricted = jnp.sum(weight * residual)
        coarse_mid = lax.psum(restricted * own_row, ("gx", "gy", "gz"))
        coarse_value = jnp.dot(own_row, coarse_mid, precision=HIGHEST)
        result = jacobi + assemble((weight * coarse_value)[None])[0]
        return (result, lax.psum(jnp.sum(weight * residual * result), ("gx", "gy", "gz")))

    pressure = jnp.zeros_like(rhs_field)
    residual = rhs_field
    direction, inner_now = precondition(residual)
    for step in range(ITERS):
        local_part = bmass * direction
        for element_which_axis in range(3):
            local_part = local_part + apply_axis(
                scaled
                * apply_axis(direction, deriv_tables[element_which_axis], element_which_axis),
                trans_tables[element_which_axis],
                element_which_axis,
            )
        image = assemble(local_part[None])[0]
        curvature = lax.psum(jnp.sum(weight * direction * image), ("gx", "gy", "gz"))
        step_size = inner_now / curvature
        pressure = pressure + step_size * direction
        residual = residual - step_size * image
        if step + 1 < ITERS:
            preconditioned, inner_next = precondition(residual)
            direction = preconditioned + inner_next / inner_now * direction
            inner_now = inner_next
    return (level_now, pressure)


def solution(mesh):
    in_specs = (
        P("gx", "gy", "gz"),
        P(None, "gx", "gy", "gz"),
        P("gx", "gy", "gz"),
        P(("gx", "gy", "gz"), None),
    )
    out_specs = (P("gx", "gy", "gz"), P("gx", "gy", "gz"))
    return jax.shard_map(body, mesh=mesh, in_specs=in_specs, out_specs=out_specs, check_vma=False)
```

profile of v0, /device:TPU:1, one launch (start us, length us, event | category | flops | bytes accessed | tf_op | source)
XLA Modules:
  0.0 2206.5 jit_solution(12459862347474892173)
XLA Ops:
  6.2 4.6 collective-permute-start
  10.8 5.5 collective-permute-start.1
  20.4 3.9 collective-permute-done.3
  30.4 3.4 collective-permute-done.5
  37.9 4.1 collective-permute-start.6
  54.7 3.6 collective-permute-start.10
  59.6 3.9 collective-permute-done.10
  63.5 5.4 collective-permute-done.11
  71.4 3.7 collective-permute-start.12
  87.6 4.9 collective-permute-start.16
  93.8 3.9 collective-permute-done.16
  97.7 3.8 collective-permute-done.17
  103.5 104.3 %psum.126 = f32[512]{0:T(512)S(1)} all-reduce(f32[512]{0:T(512)S(1)} %broadcast_multiply_fusion.13), channel_id=1, replica_groups=mesh['gx'=8,'gy'=4,'gz'=16] {'gx','gy','gz'}, use_global_device_ids=true, to_apply=%region_1.2 | all-reduce | flops 512 | bytes 4096 | tf_op jit(solution)/shard_map/psum | solution.py:172
  223.2 4.0 collective-permute-start.20
  231.8 3.9 collective-permute-start.22
  240.6 4.4 collective-permute-done.23
  247.7 3.5 collective-permute-start.30
  256.2 4.3 collective-permute-start.32
  269.5 3.9 collective-permute-done.34
  273.4 4.8 collective-permute-done.35
  279.6 104.5 %all-reduce = (f32[]{:T(128)}, f32[]{:T(128)}) all-reduce(f32[]{:T(128)} %get-tuple-element.9, f32[]{:T(128)} %get-tuple-element.8), channel_id=1, replica_groups=mesh['gx'=8,'gy'=4,'gz'=16] {'gx','gy','gz'}, use_global_device_ids=true, to_apply=%region_3.4 | all-reduce | flops 2 | bytes 16 | tf_op jit(solution)/shard_map/psum | solution.py:175
  386.8 98.4 %psum.129 = f32[512]{0:T(512)S(1)} all-reduce(f32[512]{0:T(512)S(1)} %broadcast_multiply_fusion.12), channel_id=1, replica_groups=mesh['gx'=8,'gy'=4,'gz'=16] {'gx','gy','gz'}, use_global_device_ids=true, to_apply=%region_7.8 | all-reduce | flops 512 | bytes 4096 | tf_op jit(solution)/shard_map/psum | solution.py:172
  497.0 3.4 collective-permute-done.39
  500.5 3.7 collective-permute-start.40
  505.5 3.7 collective-permute-done.40
  509.2 3.9 collective-permute-done.41
  514.5 101.3 %psum.130 = f32[]{:T(128)} all-reduce(f32[]{:T(128)} %get-tuple-element.36), channel_id=1, replica_groups=mesh['gx'=8,'gy'=4,'gz'=16] {'gx','gy','gz'}, use_global_device_ids=true, to_apply=%region_9.10 | all-reduce | flops 1 | bytes 8 | tf_op jit(solution)/shard_map/psum | solution.py:175
  636.6 3.9 collective-permute-done.46
  640.5 3.8 collective-permute-done.47
  645.7 102.2 %psum.131 = f32[]{:T(128)} all-reduce(f32[]{:T(128)} %get-tuple-element.34), channel_id=1, replica_groups=mesh['gx'=8,'gy'=4,'gz'=16] {'gx','gy','gz'}, use_global_device_ids=true, to_apply=%region_11.12 | all-reduce | flops 1 | bytes 8 | tf_op jit(solution)/shard_map/psum | solution.py:190
  750.5 99.1 %psum.132 = f32[512]{0:T(512)S(1)} all-reduce(f32[512]{0:T(512)S(1)} %broadcast_multiply_fusion.11), channel_id=1, replica_groups=mesh['gx'=8,'gy'=4,'gz'=16] {'gx','gy','gz'}, use_global_device_ids=true, to_apply=%region_13.14 | all-reduce | flops 512 | bytes 4096 | tf_op jit(solution)/shard_map/psum | solution.py:172
  861.8 3.4 collective-permute-done.51
  865.3 3.7 collective-permute-start.52
  870.3 3.7 collective-permute-done.52
  874.0 3.9 collective-permute-done.53
  879.3 100.7 %psum.133 = f32[]{:T(128)} all-reduce(f32[]{:T(128)} %get-tuple-element.30), channel_id=1, replica_groups=mesh['gx'=8,'gy'=4,'gz'=16] {'gx','gy','gz'}, use_global_device_ids=true, to_apply=%region_15.16 | all-reduce | flops 1 | bytes 8 | tf_op jit(solution)/shard_map/psum | solution.py:175
  1000.7 3.9 collective-permute-done.58
  1004.6 3.8 collective-permute-done.59
  1009.8 102.3 %psum.134 = f32[]{:T(128)} all-reduce(f32[]{:T(128)} %get-tuple-element.28), channel_id=1, replica_groups=mesh['gx'=8,'gy'=4,'gz'=16] {'gx','gy','gz'}, use_global_device_ids=true, to_apply=%region_17.18 | all-reduce | flops 1 | bytes 8 | tf_op jit(solution)/shard_map/psum | solution.py:190
  1114.7 98.7 %psum.135 = f32[512]{0:T(512)S(1)} all-reduce(f32[512]{0:T(512)S(1)} %broadcast_multiply_fusion.10), channel_id=1, replica_groups=mesh['gx'=8,'gy'=4,'gz'=16] {'gx','gy','gz'}, use_global_device_ids=true, to_apply=%region_19.20 | all-reduce | flops 512 | bytes 4096 | tf_op jit(solution)/shard_map/psum | solution.py:172
  1225.6 3.4 collective-permute-done.63
  1229.1 3.7 collective-permute-start.64
  1234.1 3.7 collective-permute-done.64
  1237.8 3.9 collective-permute-done.65
  1243.1 100.7 %psum.136 = f32[]{:T(128)} all-reduce(f32[]{:T(128)} %get-tuple-element.24), channel_id=1, replica_groups=mesh['gx'=8,'gy'=4,'gz'=16] {'gx','gy','gz'}, use_global_device_ids=true, to_apply=%region_21.22 | all-reduce | flops 1 | bytes 8 | tf_op jit(solution)/shard_map/psum | solution.py:175
  1364.5 3.9 collective-permute-done.70
  1368.4 3.8 collective-permute-done.71
  1373.6 102.5 %psum.137 = f32[]{:T(128)} all-reduce(f32[]{:T(128)} %get-tuple-element.22), channel_id=1, replica_groups=mesh['gx'=8,'gy'=4,'gz'=16] {'gx','gy','gz'}, use_global_device_ids=true, to_apply=%region_23.24 | all-reduce | flops 1 | bytes 8 | tf_op jit(solution)/shard_map/psum | solution.py:190
  1478.7 98.7 %psum.138 = f32[512]{0:T(512)S(1)} all-reduce(f32[512]{0:T(512)S(1)} %broadcast_multiply_fusion.9), channel_id=1, replica_groups=mesh['gx'=8,'gy'=4,'gz'=16] {'gx','gy','gz'}, use_global_device_ids=true, to_apply=%region_25.26 | all-reduce | flops 512 | bytes 4096 | tf_op jit(solution)/shard_map/psum | solution.py:172
  1593.1 3.7 collective-permute-start.76
  1598.1 3.7 collective-permute-done.76
  1601.8 3.9 collective-permute-done.77
  1607.0 100.7 %psum.139 = f32[]{:T(128)} all-reduce(f32[]{:T(128)} %get-tuple-element.18), channel_id=1, replica_groups=mesh['gx'=8,'gy'=4,'gz'=16] {'gx','gy','gz'}, use_global_device_ids=true, to_apply=%region_27.28 | all-reduce | flops 1 | bytes 8 | tf_op jit(solution)/shard_map/psum | solution.py:175
  1728.4 3.9 collective-permute-done.82
  1732.3 3.8 collective-permute-done.83
  1737.5 102.3 %psum.140 = f32[]{:T(128)} all-reduce(f32[]{:T(128)} %get-tuple-element.16), channel_id=1, replica_groups=mesh['gx'=8,'gy'=4,'gz'=16] {'gx','gy','gz'}, use_global_device_ids=true, to_apply=%region_29.30 | all-reduce | flops 1 | bytes 8 | tf_op jit(solution)/shard_map/psum | solution.py:190
  1842.5 98.7 %psum.141 = f32[512]{0:T(512)S(1)} all-reduce(f32[512]{0:T(512)S(1)} %broadcast_multiply_fusion.8), channel_id=1, replica_groups=mesh['gx'=8,'gy'=4,'gz'=16] {'gx','gy','gz'}, use_global_device_ids=true, to_apply=%region_31.32 | all-reduce | flops 512 | bytes 4096 | tf_op jit(solution)/shard_map/psum | solution.py:172
  1956.9 3.7 collective-permute-start.88
  1961.9 3.7 collective-permute-done.88
  1965.6 3.9 collective-permute-done.89
  1970.8 100.7 %psum.142 = f32[]{:T(128)} all-reduce(f32[]{:T(128)} %get-tuple-element.12), channel_id=1, replica_groups=mesh['gx'=8,'gy'=4,'gz'=16] {'gx','gy','gz'}, use_global_device_ids=true, to_apply=%region_33.34 | all-reduce | flops 1 | bytes 8 | tf_op jit(solution)/shard_map/psum | solution.py:175
  2092.3 3.9 collective-permute-done.94
  2096.2 3.8 collective-permute-done.95
  2102.2 102.1 %psum.143 = f32[]{:T(128)} all-reduce(f32[]{:T(128)} %fusion.92), channel_id=1, replica_groups=mesh['gx'=8,'gy'=4,'gz'=16] {'gx','gy','gz'}, use_global_device_ids=true, to_apply=%region_35.36 | all-reduce | flops 1 | bytes 8 | tf_op jit(solution)/shard_map/psum | solution.py:190
  (397 shorter events, 285.7 us)
Async XLA Ops:
  6.2 10.1 collective-permute-start
  10.8 6.3 collective-permute-start.1
  19.1 5.2 collective-permute-start.3
  25.1 4.8 collective-permute-start.4
  28.6 5.2 collective-permute-start.5
  37.9 6.1 collective-permute-start.6
  42.0 5.0 collective-permute-start.7
  54.7 8.8 collective-permute-start.10
  58.3 10.6 collective-permute-start.11
  71.4 5.7 collective-permute-start.12
  75.2 5.0 collective-permute-start.13
  87.6 10.1 collective-permute-start.16
  92.5 9.1 collective-permute-start.17
  209.1 10.4 collective-permute-start.24
  211.1 8.4 collective-permute-start.25
  214.4 8.8 collective-permute-start.18
  217.6 5.6 collective-permute-start.19
  219.6 9.2 collective-permute-start.26
  221.9 6.8 collective-permute-start.27
  223.2 8.3 collective-permute-start.20
  228.9 8.1 collective-permute-start.28
  230.2 8.5 collective-permute-start.29
  231.8 8.8 collective-permute-start.22
  235.7 9.3 collective-permute-start.23
  247.7 5.5 collective-permute-start.30
  251.3 5.0 collective-permute-start.31
  256.2 5.6 collective-permute-start.32
  265.1 8.3 collective-permute-start.34
  268.2 10.0 collective-permute-start.35
  489.3 5.0 collective-permute-start.37
  495.7 4.7 collective-permute-start.39
  500.5 8.7 collective-permute-start.40
  504.2 8.9 collective-permute-start.41
  621.0 5.0 collective-permute-start.43
  632.6 7.9 collective-permute-start.46
  635.3 9.1 collective-permute-start.47
  851.0 5.0 collective-permute-start.48
  854.0 5.0 collective-permute-start.49
  865.3 8.7 collective-permute-start.52
  869.0 8.9 collective-permute-start.53
  985.3 5.0 collective-permute-start.55
  996.9 7.7 collective-permute-start.58
  999.4 9.1 collective-permute-start.59
  1214.8 5.0 collective-permute-start.60
  1217.8 5.0 collective-permute-start.61
  1229.1 8.7 collective-permute-start.64
  1232.8 8.9 collective-permute-start.65
  1349.1 5.0 collective-permute-start.67
  1360.7 7.7 collective-permute-start.70
  1363.2 9.1 collective-permute-start.71
  1578.8 5.0 collective-permute-start.72
  1581.8 5.0 collective-permute-start.73
  1593.1 8.7 collective-permute-start.76
  1596.8 8.9 collective-permute-start.77
  1713.1 5.0 collective-permute-start.79
  1724.7 7.7 collective-permute-start.82
  1727.1 9.1 collective-permute-start.83
  1942.5 5.0 collective-permute-start.84
  1945.6 5.0 collective-permute-start.85
  1956.9 8.7 collective-permute-start.88
  1960.6 8.9 collective-permute-start.89
  2076.8 5.0 collective-permute-start.91
  2088.5 7.8 collective-permute-start.94
  2091.0 9.1 collective-permute-start.95
  (41 other events, 373.7 us)
where the time goes:
time: 2220 us; the launch traced here: 2210 us
  blocking collectives  1720 us (77%)
  starting transfers between devices  211 us (10%)
  waiting for transfers between devices  199 us (9%)
  other arithmetic  36.4 us (2%)
    psum x6, blocking collectives, precondition(): lax.psum(jnp.sum(weight * residual * result), ('gx', 'gy', 'gz'))  609 us
    psum x6, blocking collectives, precondition(): coarse_mid = lax.psum(restricted * own_row, ('gx', 'gy', 'gz'))  598 us
    psum x5, blocking collectives, body(): lax.psum(jnp.sum(weight * direction * image), ('gx', 'gy', 'gz'))  511 us
    ppermute x48, waiting for transfers between devices, extended(): lax.ppermute(head, axis, [((i + 1) % count, i) for i in range(ends)])  147 us
    ppermute x48, starting transfers between devices, extended(): lax.ppermute(tail, axis, [(i, (i + 1) % count) for i in range(ends)])  133 us
    ppermute x48, starting transfers between devices, extended(): lax.ppermute(head, axis, [((i + 1) % count, i) for i in range(ends)])  77.4 us
    ppermute x48, waiting for transfers between devices, extended(): lax.ppermute(tail, axis, [(i, (i + 1) % count) for i in range(ends)])  51.5 us
  transfers between devices with their start and end apart: 96, of which 59 were waited for; matrix products, arithmetic and copies ran while one was open for 0% of the time, Pallas kernels for 0%

commit v1 on v0

--- a/solution.py
+++ b/solution.py
@@ -169,7 +169,9 @@
     def precondition(residual):
         jacobi = residual / diagonal
         restricted = jnp.sum(weight * residual)
-        coarse_mid = lax.psum(restricted * own_row, ("gx", "gy", "gz"))
+        coarse_mid = restricted * own_row
+        for over in ("gx", ("gy", "gz")):
+            coarse_mid = lax.psum(coarse_mid, over)
         coarse_value = jnp.dot(own_row, coarse_mid, precision=HIGHEST)
         result = jacobi + assemble((weight * coarse_value)[None])[0]
         return (result, lax.psum(jnp.sum(weight * residual * result), ("gx", "gy", "gz")))

time: 2220 us -> 2490 us (1.12)
  starting transfers between devices: 211 us -> 370 us
  blocking collectives: 1720 us -> 1840 us
    ppermute x48, starting transfers between devices: 133 us -> 289 us  [extended(): lax.ppermute(tail, axis, [(i, (i + 1) % count) for i in range(ends)])]
    psum x6 -> x12, blocking collectives: 598 us -> 747 us  [precondition(): coarse_mid = lax.psum(coarse_mid, over)]
  transfers between devices with their start and end apart: 96 -> 96, of which waited for: 59 -> 60; matrix products, arithmetic and copies ran while one was open for 0% -> 0% of each run, Pallas kernels for 0% -> 0%
where the time goes in v1:
time: 2490 us; the launch traced here: 2480 us
  blocking collectives  1840 us (74%)
  starting transfers between devices  370 us (15%)
  waiting for transfers between devices  190 us (8%)
  other arithmetic  36.4 us (1%)
    psum x12, blocking collectives, precondition(): coarse_mid = lax.psum(coarse_mid, over)  747 us
    psum x6, blocking collectives, precondition(): lax.psum(jnp.sum(weight * residual * result), ('gx', 'gy', 'gz'))  592 us
    psum x5, blocking collectives, body(): lax.psum(jnp.sum(weight * direction * image), ('gx', 'gy', 'gz'))  503 us
    ppermute x48, starting transfers between devices, extended(): lax.ppermute(tail, axis, [(i, (i + 1) % count) for i in range(ends)])  289 us
    ppermute x48, waiting for transfers between devices, extended(): lax.ppermute(head, axis, [((i + 1) % count, i) for i in range(ends)])  143 us
    ppermute x48, starting transfers between devices, extended(): lax.ppermute(head, axis, [((i + 1) % count, i) for i in range(ends)])  80.7 us
  transfers between devices with their start and end apart: 96, of which 60 were waited for; matrix products, arithmetic and copies ran while one was open for 0% of the time, Pallas kernels for 0%

profile of v1, /device:TPU:1, one launch (start us, length us, event | category | flops | bytes accessed | tf_op | source)
XLA Modules:
  0.0 2480.3 jit_solution(3534614058147929920)
XLA Ops:
  6.2 4.6 collective-permute-start
  10.8 5.5 collective-permute-start.1
  20.4 3.9 collective-permute-done.3
  37.9 4.1 collective-permute-start.6
  59.6 3.9 collective-permute-done.10
  63.5 5.4 collective-permute-done.11
  71.4 3.8 collective-permute-start.12
  87.6 4.9 collective-permute-start.16
  93.8 3.9 collective-permute-done.16
  97.7 3.8 collective-permute-done.17
  103.5 12.4 psum.168
  116.0 112.0 %psum.169 = f32[512]{0:T(512)S(1)} all-reduce(f32[512]{0:T(512)S(1)} %psum.168), channel_id=1, replica_groups=mesh['gx'=8,'gy'=4,'gz'=16] {'gy','gz'}, use_global_device_ids=true, to_apply=%region_2.3 | all-reduce | flops 512 | bytes 4096 | tf_op jit(solution)/shard_map/psum | solution.py:174
  229.3 29.3 %collective-permute-start.24 = (f32[1,1,16,128]{3,1,2,0:T(1,128)S(1)}, f32[1,1,16,128]{3,1,2,0:T(1,128)S(1)}, u32[]{:S(2)}, u32[]{:S(2)}) collective-permute-start(f32[1,1,16,128]{3,1,2,0:T(1,128)S(1)} %get-tuple-element.143), channel_id=1, source_target_pairs={{0,64},{64,128},{128,192},{192,256},{256,320},{320,384},{384,448},... | collective-permute-start | bytes 24584 | tf_op jit(solution)/shard_map/ppermute | solution.py:46
  278.3 3.9 collective-permute-start.22
  287.0 3.8 collective-permute-done.23
  293.5 4.2 collective-permute-start.30
  302.7 4.3 collective-permute-start.32
  314.6 3.9 collective-permute-done.34
  318.5 3.8 collective-permute-done.35
  323.7 99.5 %all-reduce = (f32[]{:T(128)}, f32[]{:T(128)}) all-reduce(f32[]{:T(128)} %get-tuple-element.9, f32[]{:T(128)} %get-tuple-element.8), channel_id=1, replica_groups=mesh['gx'=8,'gy'=4,'gz'=16] {'gx','gy','gz'}, use_global_device_ids=true, to_apply=%region_4.5 | all-reduce | flops 2 | bytes 16 | tf_op jit(solution)/shard_map/psum | solution.py:177
  425.9 12.4 psum.172
  438.3 112.7 %psum.173 = f32[512]{0:T(512)S(1)} all-reduce(f32[512]{0:T(512)S(1)} %psum.172), channel_id=1, replica_groups=mesh['gx'=8,'gy'=4,'gz'=16] {'gy','gz'}, use_global_device_ids=true, to_apply=%region_9.10 | all-reduce | flops 512 | bytes 4096 | tf_op jit(solution)/shard_map/psum | solution.py:174
  552.4 28.6 %collective-permute-start.36 = (f32[1,1,16,128]{3,1,2,0:T(1,128)S(1)}, f32[1,1,16,128]{3,1,2,0:T(1,128)S(1)}, u32[]{:S(2)}, u32[]{:S(2)}) collective-permute-start(f32[1,1,16,128]{3,1,2,0:T(1,128)S(1)} %get-tuple-element.137), channel_id=1, source_target_pairs={{0,64},{64,128},{128,192},{192,256},{256,320},{320,384},{384,448},... | collective-permute-start | bytes 24584 | tf_op jit(solution)/shard_map/ppermute | solution.py:46
  598.2 3.8 collective-permute-done.41
  603.3 98.1 %psum.174 = f32[]{:T(128)} all-reduce(f32[]{:T(128)} %get-tuple-element.36), channel_id=1, replica_groups=mesh['gx'=8,'gy'=4,'gz'=16] {'gx','gy','gz'}, use_global_device_ids=true, to_apply=%region_11.12 | all-reduce | flops 1 | bytes 8 | tf_op jit(solution)/shard_map/psum | solution.py:177
  719.4 3.7 collective-permute-start.46
  724.4 3.7 collective-permute-done.46
  728.1 3.9 collective-permute-done.47
  733.3 100.6 %psum.175 = f32[]{:T(128)} all-reduce(f32[]{:T(128)} %get-tuple-element.34), channel_id=1, replica_groups=mesh['gx'=8,'gy'=4,'gz'=16] {'gx','gy','gz'}, use_global_device_ids=true, to_apply=%region_13.14 | all-reduce | flops 1 | bytes 8 | tf_op jit(solution)/shard_map/psum | solution.py:192
  836.6 12.4 psum.176
  849.0 111.9 %psum.177 = f32[512]{0:T(512)S(1)} all-reduce(f32[512]{0:T(512)S(1)} %psum.176), channel_id=1, replica_groups=mesh['gx'=8,'gy'=4,'gz'=16] {'gy','gz'}, use_global_device_ids=true, to_apply=%region_16.17 | all-reduce | flops 512 | bytes 4096 | tf_op jit(solution)/shard_map/psum | solution.py:174
  962.3 28.9 %collective-permute-start.48 = (f32[1,1,16,128]{3,1,2,0:T(1,128)S(1)}, f32[1,1,16,128]{3,1,2,0:T(1,128)S(1)}, u32[]{:S(2)}, u32[]{:S(2)}) collective-permute-start(f32[1,1,16,128]{3,1,2,0:T(1,128)S(1)} %get-tuple-element.133), channel_id=1, source_target_pairs={{0,64},{64,128},{128,192},{192,256},{256,320},{320,384},{384,448},... | collective-permute-start | bytes 24584 | tf_op jit(solution)/shard_map/ppermute | solution.py:46
  1008.9 3.8 collective-permute-done.53
  1014.0 98.6 %psum.178 = f32[]{:T(128)} all-reduce(f32[]{:T(128)} %get-tuple-element.30), channel_id=1, replica_groups=mesh['gx'=8,'gy'=4,'gz'=16] {'gx','gy','gz'}, use_global_device_ids=true, to_apply=%region_18.19 | all-reduce | flops 1 | bytes 8 | tf_op jit(solution)/shard_map/psum | solution.py:177
  1130.3 3.7 collective-permute-start.58
  1135.3 3.7 collective-permute-done.58
  1139.0 3.9 collective-permute-done.59
  1144.2 100.6 %psum.179 = f32[]{:T(128)} all-reduce(f32[]{:T(128)} %get-tuple-element.28), channel_id=1, replica_groups=mesh['gx'=8,'gy'=4,'gz'=16] {'gx','gy','gz'}, use_global_device_ids=true, to_apply=%region_20.21 | all-reduce | flops 1 | bytes 8 | tf_op jit(solution)/shard_map/psum | solution.py:192
  1247.5 12.4 psum.180
  1259.9 111.9 %psum.181 = f32[512]{0:T(512)S(1)} all-reduce(f32[512]{0:T(512)S(1)} %psum.180), channel_id=1, replica_groups=mesh['gx'=8,'gy'=4,'gz'=16] {'gy','gz'}, use_global_device_ids=true, to_apply=%region_23.24 | all-reduce | flops 512 | bytes 4096 | tf_op jit(solution)/shard_map/psum | solution.py:174
  1373.2 28.9 %collective-permute-start.60 = (f32[1,1,16,128]{3,1,2,0:T(1,128)S(1)}, f32[1,1,16,128]{3,1,2,0:T(1,128)S(1)}, u32[]{:S(2)}, u32[]{:S(2)}) collective-permute-start(f32[1,1,16,128]{3,1,2,0:T(1,128)S(1)} %get-tuple-element.129), channel_id=1, source_target_pairs={{0,64},{64,128},{128,192},{192,256},{256,320},{320,384},{384,448},... | collective-permute-start | bytes 24584 | tf_op jit(solution)/shard_map/ppermute | solution.py:46
  1419.8 3.8 collective-permute-done.65
  1424.9 98.4 %psum.182 = f32[]{:T(128)} all-reduce(f32[]{:T(128)} %get-tuple-element.24), channel_id=1, replica_groups=mesh['gx'=8,'gy'=4,'gz'=16] {'gx','gy','gz'}, use_global_device_ids=true, to_apply=%region_25.26 | all-reduce | flops 1 | bytes 8 | tf_op jit(solution)/shard_map/psum | solution.py:177
  1541.0 3.7 collective-permute-start.70
  1546.0 3.7 collective-permute-done.70
  1549.7 3.9 collective-permute-done.71
  1554.9 100.6 %psum.183 = f32[]{:T(128)} all-reduce(f32[]{:T(128)} %get-tuple-element.22), channel_id=1, replica_groups=mesh['gx'=8,'gy'=4,'gz'=16] {'gx','gy','gz'}, use_global_device_ids=true, to_apply=%region_27.28 | all-reduce | flops 1 | bytes 8 | tf_op jit(solution)/shard_map/psum | solution.py:192
  1658.2 12.4 psum.184
  1670.6 111.9 %psum.185 = f32[512]{0:T(512)S(1)} all-reduce(f32[512]{0:T(512)S(1)} %psum.184), channel_id=1, replica_groups=mesh['gx'=8,'gy'=4,'gz'=16] {'gy','gz'}, use_global_device_ids=true, to_apply=%region_30.31 | all-reduce | flops 512 | bytes 4096 | tf_op jit(solution)/shard_map/psum | solution.py:174
  1783.9 28.9 %collective-permute-start.72 = (f32[1,1,16,128]{3,1,2,0:T(1,128)S(1)}, f32[1,1,16,128]{3,1,2,0:T(1,128)S(1)}, u32[]{:S(2)}, u32[]{:S(2)}) collective-permute-start(f32[1,1,16,128]{3,1,2,0:T(1,128)S(1)} %get-tuple-element.125), channel_id=1, source_target_pairs={{0,64},{64,128},{128,192},{192,256},{256,320},{320,384},{384,448},... | collective-permute-start | bytes 24584 | tf_op jit(solution)/shard_map/ppermute | solution.py:46
  1830.5 3.8 collective-permute-done.77
  1835.6 98.7 %psum.186 = f32[]{:T(128)} all-reduce(f32[]{:T(128)} %get-tuple-element.18), channel_id=1, replica_groups=mesh['gx'=8,'gy'=4,'gz'=16] {'gx','gy','gz'}, use_global_device_ids=true, to_apply=%region_32.33 | all-reduce | flops 1 | bytes 8 | tf_op jit(solution)/shard_map/psum | solution.py:177
  1951.9 3.7 collective-permute-start.82
  1960.6 3.9 collective-permute-done.83
  1965.9 100.6 %psum.187 = f32[]{:T(128)} all-reduce(f32[]{:T(128)} %get-tuple-element.16), channel_id=1, replica_groups=mesh['gx'=8,'gy'=4,'gz'=16] {'gx','gy','gz'}, use_global_device_ids=true, to_apply=%region_34.35 | all-reduce | flops 1 | bytes 8 | tf_op jit(solution)/shard_map/psum | solution.py:192
  2069.1 12.4 psum.188
  2081.6 111.9 %psum.189 = f32[512]{0:T(512)S(1)} all-reduce(f32[512]{0:T(512)S(1)} %psum.188), channel_id=1, replica_groups=mesh['gx'=8,'gy'=4,'gz'=16] {'gy','gz'}, use_global_device_ids=true, to_apply=%region_37.38 | all-reduce | flops 512 | bytes 4096 | tf_op jit(solution)/shard_map/psum | solution.py:174
  2194.8 28.9 %collective-permute-start.84 = (f32[1,1,16,128]{3,1,2,0:T(1,128)S(1)}, f32[1,1,16,128]{3,1,2,0:T(1,128)S(1)}, u32[]{:S(2)}, u32[]{:S(2)}) collective-permute-start(f32[1,1,16,128]{3,1,2,0:T(1,128)S(1)} %get-tuple-element.121), channel_id=1, source_target_pairs={{0,64},{64,128},{128,192},{192,256},{256,320},{320,384},{384,448},... | collective-permute-start | bytes 24584 | tf_op jit(solution)/shard_map/ppermute | solution.py:46
  2241.4 3.8 collective-permute-done.89
  2246.5 98.4 %psum.190 = f32[]{:T(128)} all-reduce(f32[]{:T(128)} %get-tuple-element.12), channel_id=1, replica_groups=mesh['gx'=8,'gy'=4,'gz'=16] {'gx','gy','gz'}, use_global_device_ids=true, to_apply=%region_39.40 | all-reduce | flops 1 | bytes 8 | tf_op jit(solution)/shard_map/psum | solution.py:177
  2362.6 3.7 collective-permute-start.94
  2367.6 3.7 collective-permute-done.94
  2371.3 3.9 collective-permute-done.95
  2377.3 100.6 %psum.191 = f32[]{:T(128)} all-reduce(f32[]{:T(128)} %fusion.92), channel_id=1, replica_groups=mesh['gx'=8,'gy'=4,'gz'=16] {'gx','gy','gz'}, use_global_device_ids=true, to_apply=%region_41.42 | all-reduce | flops 1 | bytes 8 | tf_op jit(solution)/shard_map/psum | solution.py:192
  (403 shorter events, 307.5 us)
Async XLA Ops:
  6.2 10.1 collective-permute-start
  10.8 6.3 collective-permute-start.1
  19.1 5.2 collective-permute-start.3
  28.6 5.2 collective-permute-start.5
  37.9 6.1 collective-permute-start.6
  42.0 5.0 collective-permute-start.7
  54.7 8.8 collective-permute-start.10
  58.3 10.6 collective-permute-start.11
  71.4 5.7 collective-permute-start.12
  75.2 5.0 collective-permute-start.13
  87.6 10.1 collective-permute-start.16
  92.5 9.1 collective-permute-start.17
  229.3 37.7 %collective-permute-start.24 = (f32[1,1,16,128]{3,1,2,0:T(1,128)S(1)}, f32[1,1,16,128]{3,1,2,0:T(1,128)S(1)}, u32[]{:S(2)}, u32[]{:S(2)}) collective-permute-start(f32[1,1,16,128]{3,1,2,0:T(1,128)S(1)} %get-tuple-element.143), channel_id=1, source_target_pairs={{0,64},{64,128},{128,192},{192,256},{256,320},{320,384},{384,448},... | collective-permute-start | bytes 24584 | tf_op jit(solution)/shard_map/ppermute | solution.py:46
  258.6 8.4 collective-permute-start.25
  261.9 7.7 collective-permute-start.18
  265.1 5.0 collective-permute-start.19
  267.0 7.9 collective-permute-start.26
  268.3 6.6 collective-permute-start.27
  270.0 7.9 collective-permute-start.20
  275.2 8.8 collective-permute-start.28
  276.7 9.2 collective-permute-start.29
  278.3 8.8 collective-permute-start.22
  282.2 8.6 collective-permute-start.23
  293.5 6.2 collective-permute-start.30
  297.7 5.0 collective-permute-start.31
  302.7 5.6 collective-permute-start.32
  311.6 6.9 collective-permute-start.34
  313.3 9.1 collective-permute-start.35
  552.4 31.7 %collective-permute-start.36 = (f32[1,1,16,128]{3,1,2,0:T(1,128)S(1)}, f32[1,1,16,128]{3,1,2,0:T(1,128)S(1)}, u32[]{:S(2)}, u32[]{:S(2)}) collective-permute-start(f32[1,1,16,128]{3,1,2,0:T(1,128)S(1)} %get-tuple-element.137), channel_id=1, source_target_pairs={{0,64},{64,128},{128,192},{192,256},{256,320},{320,384},{384,448},... | collective-permute-start | bytes 24584 | tf_op jit(solution)/shard_map/ppermute | solution.py:46
  581.0 5.0 collective-permute-start.37
  591.9 6.3 collective-permute-start.40
  593.8 8.2 collective-permute-start.41
  704.6 5.6 collective-permute-start.42
  708.2 5.0 collective-permute-start.43
  719.4 8.7 collective-permute-start.46
  723.1 8.9 collective-permute-start.47
  962.3 31.6 %collective-permute-start.48 = (f32[1,1,16,128]{3,1,2,0:T(1,128)S(1)}, f32[1,1,16,128]{3,1,2,0:T(1,128)S(1)}, u32[]{:S(2)}, u32[]{:S(2)}) collective-permute-start(f32[1,1,16,128]{3,1,2,0:T(1,128)S(1)} %get-tuple-element.133), channel_id=1, source_target_pairs={{0,64},{64,128},{128,192},{192,256},{256,320},{320,384},{384,448},... | collective-permute-start | bytes 24584 | tf_op jit(solution)/shard_map/ppermute | solution.py:46
  991.2 5.0 collective-permute-start.49
  1002.1 6.8 collective-permute-start.52
  1004.5 8.2 collective-permute-start.53
  1115.8 5.2 collective-permute-start.54
  1119.1 5.0 collective-permute-start.55
  1130.3 8.7 collective-permute-start.58
  1134.0 8.9 collective-permute-start.59
  1373.2 31.6 %collective-permute-start.60 = (f32[1,1,16,128]{3,1,2,0:T(1,128)S(1)}, f32[1,1,16,128]{3,1,2,0:T(1,128)S(1)}, u32[]{:S(2)}, u32[]{:S(2)}) collective-permute-start(f32[1,1,16,128]{3,1,2,0:T(1,128)S(1)} %get-tuple-element.129), channel_id=1, source_target_pairs={{0,64},{64,128},{128,192},{192,256},{256,320},{320,384},{384,448},... | collective-permute-start | bytes 24584 | tf_op jit(solution)/shard_map/ppermute | solution.py:46
  1402.1 5.0 collective-permute-start.61
  1413.0 6.8 collective-permute-start.64
  1415.4 8.2 collective-permute-start.65
  1526.5 5.2 collective-permute-start.66
  1529.8 5.0 collective-permute-start.67
  1541.0 8.7 collective-permute-start.70
  1544.7 8.9 collective-permute-start.71
  1783.9 31.6 %collective-permute-start.72 = (f32[1,1,16,128]{3,1,2,0:T(1,128)S(1)}, f32[1,1,16,128]{3,1,2,0:T(1,128)S(1)}, u32[]{:S(2)}, u32[]{:S(2)}) collective-permute-start(f32[1,1,16,128]{3,1,2,0:T(1,128)S(1)} %get-tuple-element.125), channel_id=1, source_target_pairs={{0,64},{64,128},{128,192},{192,256},{256,320},{320,384},{384,448},... | collective-permute-start | bytes 24584 | tf_op jit(solution)/shard_map/ppermute | solution.py:46
  1823.7 6.8 collective-permute-start.76
  1826.1 8.2 collective-permute-start.77
  1937.4 5.2 collective-permute-start.78
  1951.9 8.7 collective-permute-start.82
  1955.6 8.9 collective-permute-start.83
  2194.8 31.6 %collective-permute-start.84 = (f32[1,1,16,128]{3,1,2,0:T(1,128)S(1)}, f32[1,1,16,128]{3,1,2,0:T(1,128)S(1)}, u32[]{:S(2)}, u32[]{:S(2)}) collective-permute-start(f32[1,1,16,128]{3,1,2,0:T(1,128)S(1)} %get-tuple-element.121), channel_id=1, source_target_pairs={{0,64},{64,128},{128,192},{192,256},{256,320},{320,384},{384,448},... | collective-permute-start | bytes 24584 | tf_op jit(solution)/shard_map/ppermute | solution.py:46
  2234.7 6.8 collective-permute-start.88
  2237.0 8.2 collective-permute-start.89
  2348.1 5.2 collective-permute-start.90
  2362.6 8.7 collective-permute-start.94
  2366.3 8.9 collective-permute-start.95
  (41 other events, 467.9 us)
